TPU v7x, 32 devices: a whole 2x2x4 slice. The times are simulated.
32 devices in a mesh: section: 4 (over y, x), tile: 8 (over z, core).
Axes of the slice: x: 2, y: 2, z: 4, core: 2. Of those that a mesh axis runs over, the one named last changes fastest.
Arguments:
- forcing: bfloat16 [262144, 128], P(('section', 'tile')), may hold values from -6 to 6
- w_in: bfloat16 [128, 1024], replicated, may hold values from -0.5 to 0.5
- bias_in: float32 [1024], replicated, may hold values from -3 to 3
- w_out: bfloat16 [1024, 128], replicated, may hold values from -0.1875 to 0.1875
- target_tile_index: int32 [262144, 1], P(('section', 'tile')), may hold values from 0 to 7; in each aligned block of 8192 rows (0 to 8191, 8192 to 16383, ...) at most 2048 rows name the same one
- reach_slot: int32 [262144], P(('section', 'tile')), may hold values from 0 to 63
- k_ratio: float32 [4, 512], P(None, ('section', 'tile')), may hold values from 1 to 40
- x_weight: float32 [4, 512], P(None, ('section', 'tile')), may hold values from 0.05 to 0.3
- down_link: int32 [4, 512], P(None, ('section', 'tile')), may hold values from 0 to 127
- cotangent: float32 [4, 512, 128], P(None, ('section', 'tile')), may hold values from -6 to 6
Outputs:
- discharge: float32 [4, 512, 128], P(None, ('section', 'tile'))
- grad_w_in: float32 [128, 1024], replicated
- grad_bias: float32 [1024], replicated
- grad_w_out: float32 [1024, 128], replicated
Inputs may be any that keep to these rules, and one draw needn't show every extreme that they name: `target_tile_index`: among the catchments of one device, at most 2048 name the same tile, a bound that some block reaches. `down_link`: entries of last-section reaches are not used.
All inputs are finite; a program needn't handle non-finite values.
Results may differ from a plain program's by a relative error of at most 0.0038.
Values may be sent and summed in bfloat16 or wider, within the bound.
A program may use at most 192 MiB of HBM per device.

v0:
```python
import jax
import jax.numpy as jnp
from jax import lax
from jax.sharding import PartitionSpec as P


def shifted(block, axis, distance):
    devices = range(lax.axis_size(axis))
    route = [(i - distance, i) for i in devices if i - distance in devices]
    return lax.ppermute(block, axis, route)


def coefficients(k_ratio, x_weight):
    storage = 2.0 * k_ratio * (1.0 - x_weight)
    denom = storage + 1.0
    c_now = (1.0 - 2.0 * k_ratio * x_weight) / denom
    c_prev = (1.0 + 2.0 * k_ratio * x_weight) / denom
    c_keep = (storage - 1.0) / denom
    c_side = 2.0 / denom
    return (c_now, c_prev, c_keep, c_side)


def linear_combine(first, second):
    return (first[0] * second[0], second[0] * first[1] + second[1])


def route(inflow, lateral, coefs):
    c_now, c_prev, c_keep, c_side = coefs
    before = jnp.pad(inflow[:, :, :-1], ((0, 0), (0, 0), (1, 0)))
    drive = c_now[:, :, None] * inflow + c_prev[:, :, None] * before + c_side[:, :, None] * lateral
    decay = jnp.broadcast_to(c_keep[:, :, None], drive.shape)
    _, outs = lax.associative_scan(linear_combine, (decay, drive), axis=2)
    return outs


def route_back(grad_out, coefs):
    c_now, c_prev, c_keep, c_side = coefs
    decay = jnp.broadcast_to(c_keep[:, :, None], grad_out.shape)
    _, adjoint = lax.associative_scan(linear_combine, (decay, grad_out), axis=2, reverse=True)
    after = jnp.pad(adjoint[:, :, 1:], ((0, 0), (0, 0), (0, 1)))
    grad_in = c_now[:, :, None] * adjoint + c_prev[:, :, None] * after
    grad_lat = c_side[:, :, None] * adjoint
    return (grad_in, grad_lat)


def reach_link_matrix(links, span):
    return (links[:, :, None] == jnp.arange(span, dtype=jnp.int32)[None, None, :]).astype(
        jnp.float32
    )


def pass_down(reach_outflow, links, span):
    lookup_matrix = reach_link_matrix(links, span)
    section_pieces = jnp.einsum(
        "zum,zuh->zmh", lookup_matrix, reach_outflow, precision=lax.Precision.HIGHEST
    )
    summed = lax.psum_scatter(
        section_pieces.astype(jnp.bfloat16), "tile", scatter_dimension=1, tiled=True
    ).astype(jnp.float32)
    return shifted(summed, "section", 1)


def pass_up(grad_in):
    moved = shifted(grad_in, "section", -1)
    return lax.all_gather(moved, "tile", axis=1, tiled=True)


def pick_rows(entire_network, links):
    lookup_matrix = reach_link_matrix(links, entire_network.shape[1])
    return jnp.einsum(
        "pox,pxc->poc", lookup_matrix, entire_network, precision=lax.Precision.HIGHEST
    )


def local(
    forcing,
    w_in,
    bias_in,
    w_out,
    target_tile_index,
    reach_slot,
    k_ratio,
    x_weight,
    down_link,
    cotangent,
):
    tiles = lax.axis_size("tile")
    river_sections = lax.axis_size("section")
    cells = forcing.shape[0]
    groups, reaches = k_ratio.shape
    steps_len = w_out.shape[1]
    span = tiles * reaches
    capacity = 2 * cells // tiles
    pre = jnp.dot(forcing, w_in, preferred_element_type=jnp.float32) + bias_in
    hidden = jax.nn.silu(pre).astype(jnp.bfloat16)
    runoff = (0.125 * jnp.dot(hidden, w_out, preferred_element_type=jnp.float32)).astype(
        jnp.bfloat16
    )
    target = target_tile_index[:, 0]
    onehot = (target[:, None] == jnp.arange(tiles, dtype=jnp.int32)[None, :]).astype(jnp.int32)
    rank = jnp.sum((jnp.cumsum(onehot, axis=0) - 1) * onehot, axis=1)
    position = target * capacity + rank
    send_rows = jnp.zeros((tiles * capacity, steps_len), jnp.bfloat16).at[position].set(runoff)
    send_ids = (
        jnp.full((tiles * capacity,), groups * reaches, jnp.int32).at[position].set(reach_slot)
    )
    recv_rows, recv_ids = (
        lax.all_to_all(send_rows, "tile", split_axis=0, concat_axis=0, tiled=True),
        lax.all_to_all(send_ids, "tile", split_axis=0, concat_axis=0, tiled=True),
    )
    buckets = (recv_ids[:, None] == jnp.arange(groups * reaches, dtype=jnp.int32)[None, :]).astype(
        jnp.bfloat16
    )
    lateral = lax.dot_general(
        buckets, recv_rows, (((0,), (0,)), ((), ())), preferred_element_type=jnp.float32
    )
    lateral = lateral.reshape(groups, reaches, steps_len)
    coefs = coefficients(k_ratio, x_weight)
    incoming = jnp.zeros((groups, reaches, steps_len), jnp.float32)
    for level in range(river_sections):
        discharge = route(incoming, lateral, coefs)
        if level + 1 < river_sections:
            incoming = pass_down(discharge, down_link, span)
    extra = jnp.zeros((groups, reaches, steps_len), jnp.float32)
    for level in range(river_sections):
        grad_in, grad_lateral = route_back(cotangent + extra, coefs)
        if level + 1 < river_sections:
            extra = pick_rows(pass_up(grad_in), down_link)
    flat = grad_lateral.reshape(groups * reaches, steps_len).astype(jnp.bfloat16)
    back_rows = jnp.dot(buckets, flat, preferred_element_type=jnp.float32).astype(jnp.bfloat16)
    returned = lax.all_to_all(back_rows, "tile", split_axis=0, concat_axis=0, tiled=True)
    grad_runoff = returned[position]
    grad_w_out = 0.125 * lax.dot_general(
        hidden, grad_runoff, (((0,), (0,)), ((), ())), preferred_element_type=jnp.float32
    )
    grad_hidden = 0.125 * lax.dot_general(
        grad_runoff, w_out, (((1,), (1,)), ((), ())), preferred_element_type=jnp.float32
    )
    sig = jax.nn.sigmoid(pre)
    grad_pre = grad_hidden * sig * (1.0 + pre * (1.0 - sig))
    grad_bias = jnp.sum(grad_pre, axis=0)
    grad_w_in = lax.dot_general(
        forcing,
        grad_pre.astype(jnp.bfloat16),
        (((0,), (0,)), ((), ())),
        preferred_element_type=jnp.float32,
    )
    grad_w_in, grad_bias, grad_w_out = lax.psum(
        (grad_w_in, grad_bias, grad_w_out), ("section", "tile")
    )
    return (discharge, grad_w_in, grad_bias, grad_w_out)


def solution(mesh):
    placed = (
        P(("section", "tile"), None),
        P(),
        P(),
        P(),
        P(("section", "tile"), None),
        P(("section", "tile")),
        P(None, ("section", "tile")),
        P(None, ("section", "tile")),
        P(None, ("section", "tile")),
        P(None, ("section", "tile"), None),
    )
    return jax.shard_map(
        local,
        mesh=mesh,
        in_specs=placed,
        out_specs=(P(None, ("section", "tile"), None), P(), P(), P()),
        check_vma=False,
    )
```

profile of v0, /device:TPU:0, one launch (start us, length us, event | category | flops | bytes accessed | tf_op | source)
XLA Modules:
  0.0 649.4 jit_solution(12011391910219636179)
XLA Ops:
  7.2 0.9 fusion.18
  8.1 2.4 reduce-window.6
  11.2 1.0 fusion.17
  12.2 0.8 compare_select_fusion
  13.0 31.2 %scatter_custom_fusion = s32[16384]{0:T(1024)} fusion(s32[8192]{0:T(1024)S(1)} %bitcast.132, s32[8192]{0:T(1024)} %param.15, s32[]{:T(128)} %constant.15.clone.1), kind=kCustom, calls=%fused_computation.251 | custom fusion | bytes 66048 | tf_op jit(solution)/shard_map/scatter | solution.py:105
  44.3 6.3 all-to-all-start
  50.6 1.4 slice.1239
  52.0 1.4 slice.1241
  58.0 19.1 %multiply_convert_fusion = (bf16[8192,1024]{1,0:T(8,128)(2,1)}, f32[8192,1024]{1,0:T(8,128)}) fusion(f32[1024]{0:T(1024)S(1)} %copy-done.7, bf16[8192,128]{1,0:T(8,128)(2,1)S(1)} %copy-done, bf16[128,1024]{1,0:T(8,128)(2,1)S(1)} %copy-done.4), kind=kOutput, calls=%fused_computation.4 | convolution fusion | flops 2197815296 | bytes 52695040 | tf_op jit(solution)/shard_map/dot_general | solution.py:94
  77.1 9.6 %fusion.2 = bf16[8192,128]{1,0:T(8,128)(2,1)} fusion(bf16[8192,1024]{1,0:T(8,128)(2,1)} %get-tuple-element.83, bf16[1024,128]{1,0:T(8,128)(2,1)S(1)} %copy-done.5), kind=kOutput, calls=%fused_computation.10 | convolution fusion | flops 2149580800 | bytes 19136512 | tf_op jit(solution)/shard_map/dot_general | solution.py:96
  86.7 24.0 %scatter_custom_fusion.1 = bf16[16384,128]{1,0:T(8,128)(2,1)} fusion(s32[8192]{0:T(1024)S(1)} %bitcast.133, bf16[8192,128]{1,0:T(8,128)(2,1)} %fusion.2, bf16[]{:T(256)} %constant.11.clone.1), kind=kCustom, calls=%fused_computation.15 | custom fusion | bytes 4194816 | tf_op jit(solution)/shard_map/scatter | solution.py:103
  110.8 5.1 all-to-all-start.1
  124.2 0.8 pad.443
  125.3 1.3 collective-permute-start.3
  126.9 4.2 collective-permute-done.3
  131.1 85.7 %all_gather.9 = f32[4,128,128]{2,1,0:T(8,128)S(1)} all-gather(f32[4,16,128]{2,1,0:T(8,128)S(1)} %collective-permute-done.3), channel_id=1, replica_groups=mesh['section'=4,'tile'=8] {'tile'}, dimensions={1}, use_global_device_ids=true | all-gather | bytes 294912 | tf_op jit(solution)/shard_map/all_gather | solution.py:65
  227.3 0.8 pad.458
  228.3 3.1 multiply_add_fusion.13
  241.0 0.8 pad.384
  242.8 1.3 collective-permute-start.4
  244.1 1.1 convolution_convert_fusion.3
  245.2 3.3 collective-permute-done.4
  248.6 14.4 %all_gather.10 = f32[4,128,128]{2,1,0:T(8,128)S(1)} all-gather(f32[4,16,128]{2,1,0:T(8,128)S(1)} %collective-permute-done.4), channel_id=1, replica_groups=mesh['section'=4,'tile'=8] {'tile'}, dimensions={1}, use_global_device_ids=true | all-gather | bytes 294912 | tf_op jit(solution)/shard_map/all_gather | solution.py:65
  273.4 0.8 pad.473
  274.2 2.8 reduce-scatter.4.cloned.1.call-done
  277.8 3.5 collective-permute-start
  281.4 1.4 collective-permute-done
  288.0 1.3 collective-permute-start.5
  293.9 0.8 pad.399
  295.7 1.1 convolution_convert_fusion.2
  296.8 14.3 %all_gather.11 = f32[4,128,128]{2,1,0:T(8,128)S(1)} all-gather(f32[4,16,128]{2,1,0:T(8,128)S(1)} %collective-permute-done.5), channel_id=1, replica_groups=mesh['section'=4,'tile'=8] {'tile'}, dimensions={1}, use_global_device_ids=true | all-gather | bytes 294912 | tf_op jit(solution)/shard_map/all_gather | solution.py:65
  322.5 5.6 reduce-scatter.6.cloned.1.call-done
  328.9 3.6 collective-permute-start.1
  332.5 4.4 convolution_convert_fusion
  336.9 4.5 all-to-all-start.2
  353.0 1.1 convolution_convert_fusion.1
  354.2 33.0 %reduce-scatter.8.cloned.1.call-done = bf16[4,16,128]{2,1,0:T(8,128)(2,1)} async-done(((bf16[4,128,128]{2,1,0:T(8,128)(2,1)}), bf16[4,16,128]{2,1,0:T(8,128)(2,1)}) %reduce-scatter.8.cloned.1.call-update) | async-done | bytes 16400 | tf_op jit(solution)/shard_map/reduce_scatter | solution.py:57
  387.9 3.4 collective-permute-start.2
  391.3 1.6 collective-permute-done.2
  401.0 35.7 %all-to-all-done.2 = bf16[8,2048,128]{2,1,0:T(8,128)(2,1)} async-done(((bf16[8,2048,128]{2,1,0:T(8,128)(2,1)}), bf16[8,2048,128]{2,1,0:T(8,128)(2,1)}, u32[]{:S(2)}, u32[]{:S(2)}) %all-to-all-start.2) | async-done | bytes 4194336 | tf_op jit(solution)/shard_map/all_to_all | solution.py:131
  436.7 30.7 %gather_fusion = bf16[8192,128]{1,0:T(8,128)(2,1)} fusion(bf16[16384,128]{1,0:T(8,128)(2,1)} %bitcast.14, s32[8192]{0:T(1024)S(1)} %broadcast_clamp_fusion), kind=kCustom, calls=%fused_computation | custom fusion | bytes 4227072 | tf_op jit(solution)/shard_map/gather | solution.py:132
  467.4 11.8 %convolution_multiply_fusion.1 = f32[1024,128]{1,0:T(8,128)} fusion(bf16[8192,1024]{1,0:T(8,128)(2,1)} %get-tuple-element.83, bf16[8192,128]{1,0:T(8,128)(2,1)} %gather_fusion), kind=kOutput, calls=%fused_computation.20 | convolution fusion | flops 2147614720 | bytes 19398656 | tf_op jit(solution)/shard_map/dot_general | solution.py:133
  479.2 21.9 %fusion.84 = (f32[1024]{0:T(1024)S(1)}, bf16[8192,1024]{1,0:T(8,128)(2,1)}) fusion(f32[8192,1024]{1,0:T(8,128)} %get-tuple-element.84, f32[1024]{0:T(1024)S(1)} %copy-done.7, bf16[8192,128]{1,0:T(8,128)(2,1)S(1)} %copy-done.1, bf16[1024,128]{1,0:T(8,128)(2,1)S(1)} %copy-done.6), kind=kOutput, calls=%fused_computation.296 | convolution fusion | flops 2248145920 | bytes 52699136 | tf_op jit(solution)/shard_map/dot_general | solution.py:136
  501.1 8.9 %fusion.10 = f32[128,1024]{0,1:T(8,128)} fusion(bf16[8192,128]{1,0:T(8,128)(2,1)S(1)} %copy-done, bf16[8192,1024]{1,0:T(8,128)(2,1)} %get-tuple-element.87), kind=kOutput, calls=%fused_computation.19 | convolution fusion | flops 2147483648 | bytes 19398656 | tf_op jit(solution)/shard_map/dot_general | solution.py:142
  514.3 37.1 %psum.22 = f32[1024]{0:T(1024)} all-reduce(f32[1024]{0:T(1024)S(1)} %get-tuple-element.86), channel_id=1, replica_groups=mesh['section'=4,'tile'=8] {'section','tile'}, use_global_device_ids=true, to_apply=%region_10.11 | all-reduce | flops 1024 | bytes 8192 | tf_op jit(solution)/shard_map/psum | solution.py:148
  551.4 87.2 %all-reduce.122.cloned.1.call-done = (f32[128,1024]{0,1:T(8,128)}, f32[1024,128]{1,0:T(8,128)}) async-done(((f32[128,1024]{0,1:T(8,128)}, f32[1024,128]{1,0:T(8,128)}), (f32[128,1024]{0,1:T(8,128)}, f32[1024,128]{1,0:T(8,128)})) %all-reduce.122.cloned.1.call-update) | async-done | bytes 1048592 | tf_op jit(solution)/shard_map/psum | solution.py:148
  638.6 2.0 copy.99
  640.6 1.9 copy.104
  (524 shorter events, 92.3 us)
Async XLA Ops:
  7.2 50.8 %copy-start = (bf16[8192,128]{1,0:T(8,128)(2,1)S(1)}, bf16[8192,128]{1,0:T(8,128)(2,1)}, u32[]{:S(2)}) copy-start(bf16[8192,128]{1,0:T(8,128)(2,1)} %param.10) | copy-start | bytes 6291460
  7.2 50.8 %copy-start.4 = (bf16[128,1024]{1,0:T(8,128)(2,1)S(1)}, bf16[128,1024]{1,0:T(8,128)(2,1)}, u32[]{:S(2)}) copy-start(bf16[128,1024]{1,0:T(8,128)(2,1)} %param.11) | copy-start | bytes 786436
  7.2 50.8 %copy-start.7 = (f32[1024]{0:T(1024)S(1)}, f32[1024]{0:T(1024)}, u32[]{:S(2)}) copy-start(f32[1024]{0:T(1024)} %param.12) | copy-start | bytes 12292
  44.3 66.5 %all-to-all-start = ((s32[8,2048,1]{1,2,0:T(1,128)}), s32[8,2048,1]{1,2,0:T(1,128)S(1)}, u32[]{:S(2)}, u32[]{:S(2)}) async-start(s32[8,2048,1]{1,2,0:T(1,128)} %bitcast.5), calls=%async_computation | async-start | bytes 131072 | tf_op jit(solution)/shard_map/all_to_all | solution.py:109
  58.0 19.1 %copy-start.5 = (bf16[1024,128]{1,0:T(8,128)(2,1)S(1)}, bf16[1024,128]{1,0:T(8,128)(2,1)}, u32[]{:S(2)}) copy-start(bf16[1024,128]{1,0:T(8,128)(2,1)} %param.13) | copy-start | bytes 786436
  110.8 7.2 %copy-start.2 = (f32[4,16,128]{2,1,0:T(8,128)S(1)}, f32[4,16,128]{2,1,0:T(8,128)}, u32[]{:S(2)}) copy-start(f32[4,16,128]{2,1,0:T(8,128)} %param.19) | copy-start | bytes 98308
  110.8 117.5 %all-to-all-start.1 = ((bf16[8,2048,128]{2,1,0:T(8,128)(2,1)}), bf16[8,2048,128]{2,1,0:T(8,128)(2,1)}, u32[]{:S(2)}, u32[]{:S(2)}) async-start(bf16[8,2048,128]{2,1,0:T(8,128)(2,1)} %bitcast.89), calls=%async_computation.1 | async-start | bytes 8388608 | tf_op jit(solution)/shard_map/all_to_all | solution.py:108
  115.9 100.9 %copy-start.3 = (s32[4,16]{1,0:T(4,128)S(1)}, s32[4,16]{1,0:T(4,128)}, u32[]{:S(2)}) copy-start(s32[4,16]{1,0:T(4,128)} %param.18) | copy-start | bytes 772
  115.9 161.2 %reduce-scatter.4.cloned.1.call-start = ((), (), s32[]{:S(2)}) async-start(), calls=%async_computation.6 | async-start | bytes 147456 | tf_op jit(solution)/shard_map/reduce_scatter | solution.py:57
  125.3 5.8 collective-permute-start.3
  242.8 5.8 collective-permute-start.4
  245.2 82.9 %reduce-scatter.6.cloned.1.call-start = ((), (), s32[]{:S(2)}) async-start(), calls=%async_computation.7 | async-start | bytes 147456 | tf_op jit(solution)/shard_map/reduce_scatter | solution.py:57
  277.8 5.1 collective-permute-start
  288.0 8.8 %collective-permute-start.5 = (f32[4,16,128]{2,1,0:T(8,128)S(1)}, f32[4,16,128]{2,1,0:T(8,128)S(1)}, u32[]{:S(2)}, u32[]{:S(2)}) collective-permute-start(f32[4,16,128]{2,1,0:T(8,128)S(1)} %get-tuple-element.69), channel_id=1, source_target_pairs={{8,0},{16,8},{24,16},{9,1},{17,9},{25,17},{10,2},{18,10},{26,18},{... | collective-permute-start | bytes 98312 | tf_op jit(solution)/shard_map/ppermute | solution.py:10
  328.9 12.6 %collective-permute-start.1 = (f32[4,16,128]{2,1,0:T(8,128)S(1)}, f32[4,16,128]{2,1,0:T(8,128)S(1)}, u32[]{:S(2)}, u32[]{:S(2)}) collective-permute-start(f32[4,16,128]{2,1,0:T(8,128)S(1)} %convert_element_type.63), channel_id=1, source_target_pairs={{0,8},{8,16},{16,24},{1,9},{9,17},{17,25},{2,10},{10,18},{18,26},{... | collective-permute-start | bytes 98312 | tf_op jit(solution)/shard_map/ppermute | solution.py:10
  336.9 99.8 %all-to-all-start.2 = ((bf16[8,2048,128]{2,1,0:T(8,128)(2,1)}), bf16[8,2048,128]{2,1,0:T(8,128)(2,1)}, u32[]{:S(2)}, u32[]{:S(2)}) async-start(bf16[8,2048,128]{2,1,0:T(8,128)(2,1)} %bitcast.88), calls=%async_computation.5 | async-start | bytes 8388608 | tf_op jit(solution)/shard_map/all_to_all | solution.py:131
  341.4 45.8 %reduce-scatter.8.cloned.1.call-start = ((), (), s32[]{:S(2)}) async-start(), calls=%async_computation.8 | async-start | bytes 147456 | tf_op jit(solution)/shard_map/reduce_scatter | solution.py:57
  354.2 284.4 %all-reduce.122.cloned.1.call-start = ((), (), s32[]{:S(2)}) async-start(), calls=%async_computation.9 | async-start | bytes 2097152 | tf_op jit(solution)/shard_map/psum | solution.py:148
  387.9 4.9 collective-permute-start.2
  467.4 11.8 %copy-start.1 = (bf16[8192,128]{1,0:T(8,128)(2,1)S(1)}, bf16[8192,128]{1,0:T(8,128)(2,1)}, u32[]{:S(2)}) copy-start(bf16[8192,128]{1,0:T(8,128)(2,1)} %gather_fusion) | copy-start | bytes 6291460
  467.4 11.8 %copy-start.6 = (bf16[1024,128]{1,0:T(8,128)(2,1)S(1)}, bf16[1024,128]{1,0:T(8,128)(2,1)}, u32[]{:S(2)}) copy-start(bf16[1024,128]{1,0:T(8,128)(2,1)} %param.13) | copy-start | bytes 786436
Sparse Core Ops, SparseCore 0:
  245.3 31.6 reduce-scatter.3
  296.9 31.1 reduce-scatter.5
  354.3 32.8 reduce-scatter.7
  510.2 128.3 all-reduce.121
where the time goes:
time: 660 us; the launch traced here: 649 us
  waiting for transfers between devices  175 us (27%)
  local copies, waits for them, and re-layouts  173 us (26%)
  blocking collectives  152 us (23%)
  matrix products  82.9 us (13%)
  starting transfers between devices  30.8 us (5%)
  other arithmetic  19.5 us (3%)
  between operations  16.7 us (3%)
    all_gather x3, blocking collectives, pass_up(): return lax.all_gather(moved, 'tile', axis=1, tiled=True)  114 us
    psum x1, waiting for transfers between devices, local(): lax.psum((grad_w_in, grad_bias, grad_w_out), ('section', 'tile'))  87.2 us
    reduce_scatter x3, waiting for transfers between devices, pass_down(): lax.psum_scatter(section_pieces.astype(jnp.bfloat16), 'tile', scatter_dim...  41.4 us
    psum x1, blocking collectives, local(): lax.psum((grad_w_in, grad_bias, grad_w_out), ('section', 'tile'))  37.1 us
    all_to_all x1, waiting for transfers between devices, local(): lax.all_to_all(back_rows, 'tile', split_axis=0, concat_axis=0, tiled=True)  35.7 us
    scatter x1, local copies, waits for them, and re-layouts, local(): jnp.full((tiles * capacity,), groups * reaches, jnp.int32).at[position]  31.2 us
    gather x1, local copies, waits for them, and re-layouts, local(): grad_runoff = returned[position]  30.7 us
    scatter x1, local copies, waits for them, and re-layouts, local(): jnp.zeros((tiles * capacity, steps_len), jnp.bfloat16).at[position]  24 us
  transfers between devices with their start and end apart: 13, of which 9 were waited for; matrix products, arithmetic and copies ran while one was open for 22% of the time, Pallas kernels for 0%

commit v1 on v0

--- a/solution.py
+++ b/solution.py
@@ -61,8 +61,33 @@
 
 
 def pass_up(grad_in):
+
+    def _prepare_layers_all(block_in, shard_axis="tile"):
+        r1 = lax.axis_index(shard_axis)
+        arr_out = lax.axis_size(shard_axis)
+        low, current_value, aux = (arr_out, r1, block_in.shape[1])
+        vals = tuple(((j0, (j0 + 1) % low) for j0 in range(low)))
+        table = tuple(((j0, (j0 - 1) % low) for j0 in range(low)))
+        heard = jnp.zeros((*block_in.shape[:1], low * aux, *block_in.shape[2:]), block_in.dtype)
+        heard = lax.dynamic_update_slice_in_dim(heard, block_in, current_value * aux, axis=1)
+        view_out = low // 2
+        mixed_arr = e_now = block_in
+        w = 1
+        while w < view_out + 1:
+            mixed_arr = lax.ppermute(mixed_arr, shard_axis, vals)
+            heard = lax.dynamic_update_slice_in_dim(
+                heard, mixed_arr, (current_value - w) % low * aux, axis=1
+            )
+            if w < low - view_out:
+                e_now = lax.ppermute(e_now, shard_axis, table)
+                heard = lax.dynamic_update_slice_in_dim(
+                    heard, e_now, (current_value + w) % low * aux, axis=1
+                )
+            w += 1
+        return heard
+
     moved = shifted(grad_in, "section", -1)
-    return lax.all_gather(moved, "tile", axis=1, tiled=True)
+    return _prepare_layers_all(moved)
 
 
 def pick_rows(entire_network, links):

time: 660 us -> 672 us (1.018)
  blocking collectives: 152 us -> 38 us
  waiting for transfers between devices: 175 us -> 251 us
  starting transfers between devices: 30.8 us -> 76.5 us
    all_gather x3 -> x0, blocking collectives: 114 us -> none  [pass_up(): return lax.all_gather(moved, 'tile', axis=1, tiled=True)]
    ppermute x0 -> x21, waiting for transfers between devices: none -> 81.8 us  [the longest x12 81.2 us: _prepare_layers_all(): mixed_arr = lax.ppermute(mixed_arr, shard_axis, vals)]
    ppermute x0 -> x21, starting transfers between devices: none -> 44.8 us  [the longest x9 29.7 us: _prepare_layers_all(): e_now = lax.ppermute(e_now, shard_axis, table)]
  transfers between devices with their start and end apart: 13 -> 34, of which waited for: 9 -> 21; matrix products, arithmetic and copies ran while one was open for 22% -> 22% of each run, Pallas kernels for 0% -> 0%
where the time goes in v1:
time: 672 us; the launch traced here: 661 us
  waiting for transfers between devices  251 us (37%)
  local copies, waits for them, and re-layouts  174 us (26%)
  matrix products  85 us (13%)
  starting transfers between devices  76.5 us (11%)
  blocking collectives  38 us (6%)
  other arithmetic  19.5 us (3%)
  between operations  16.8 us (2%)
    psum x1, waiting for transfers between devices, local(): lax.psum((grad_w_in, grad_bias, grad_w_out), ('section', 'tile'))  87.6 us
    ppermute x12, waiting for transfers between devices, _prepare_layers_all(): mixed_arr = lax.ppermute(mixed_arr, shard_axis, vals)  81.2 us
    reduce_scatter x3, waiting for transfers between devices, pass_down(): lax.psum_scatter(section_pieces.astype(jnp.bfloat16), 'tile', scatter_dim...  38.9 us
    psum x1, blocking collectives, local(): lax.psum((grad_w_in, grad_bias, grad_w_out), ('section', 'tile'))  38 us
    all_to_all x1, waiting for transfers between devices, local(): lax.all_to_all(back_rows, 'tile', split_axis=0, concat_axis=0, tiled=True)  34.4 us
    scatter x1, local copies, waits for them, and re-layouts, local(): jnp.full((tiles * capacity,), groups * reaches, jnp.int32).at[position]  31.2 us
    gather x1, local copies, waits for them, and re-layouts, local(): grad_runoff = returned[position]  30.7 us
    ppermute x9, starting transfers between devices, _prepare_layers_all(): e_now = lax.ppermute(e_now, shard_axis, table)  29.7 us
  transfers between devices with their start and end apart: 34, of which 21 were waited for; matrix products, arithmetic and copies ran while one was open for 22% of the time, Pallas kernels for 0%

profile of v1, /device:TPU:0, one launch (start us, length us, event | category | flops | bytes accessed | tf_op | source)
XLA Modules:
  0.0 661.2 jit_solution(3662277187224734019)
XLA Ops:
  8.1 2.4 reduce-window.6
  13.0 31.2 %scatter_custom_fusion = s32[16384]{0:T(1024)} fusion(s32[8192]{0:T(1024)S(1)} %bitcast.132, s32[8192]{0:T(1024)} %param.15, s32[]{:T(128)} %constant.105.clone.1), kind=kCustom, calls=%fused_computation.251 | custom fusion | bytes 66048 | tf_op jit(solution)/shard_map/scatter | solution.py:130
  44.3 6.3 all-to-all-start
  61.4 19.1 %multiply_convert_fusion = (bf16[8192,1024]{1,0:T(8,128)(2,1)}, f32[8192,1024]{1,0:T(8,128)}) fusion(f32[1024]{0:T(1024)S(1)} %copy-done.6, bf16[8192,128]{1,0:T(8,128)(2,1)S(1)} %copy-done, bf16[128,1024]{1,0:T(8,128)(2,1)S(1)} %copy-done.4), kind=kOutput, calls=%fused_computation.4 | convolution fusion | flops 2197815296 | bytes 52695040 | tf_op jit(solution)/shard_map/dot_general | solution.py:119
  80.5 11.6 %fusion.2 = bf16[8192,128]{1,0:T(8,128)(2,1)} fusion(bf16[8192,1024]{1,0:T(8,128)(2,1)} %get-tuple-element.83, bf16[1024,128]{1,0:T(8,128)(2,1)} %param.13), kind=kOutput, calls=%fused_computation.10 | convolution fusion | flops 2149580800 | bytes 19136512 | tf_op jit(solution)/shard_map/dot_general | solution.py:121
  92.2 24.2 %scatter_custom_fusion.1 = bf16[16384,128]{1,0:T(8,128)(2,1)} fusion(s32[8192]{0:T(1024)S(1)} %bitcast.133, bf16[8192,128]{1,0:T(8,128)(2,1)} %fusion.2, bf16[]{:T(256)} %constant.111.clone.1), kind=kCustom, calls=%fused_computation.15 | custom fusion | bytes 4194816 | tf_op jit(solution)/shard_map/scatter | solution.py:128
  116.4 5.1 all-to-all-start.1
  128.9 4.1 collective-permute-done.3
  133.0 3.5 collective-permute-start.5
  136.6 57.8 %collective-permute-done.4 = f32[4,16,128]{2,1,0:T(8,128)S(1)} collective-permute-done((f32[4,16,128]{2,1,0:T(8,128)S(1)}, f32[4,16,128]{2,1,0:T(8,128)S(1)}, u32[]{:S(2)}, u32[]{:S(2)}) %collective-permute-start.4) | collective-permute-done | bytes 32800 | tf_op jit(solution)/shard_map/ppermute | solution.py:77
  194.3 3.5 collective-permute-start.7
  197.9 1.7 collective-permute-done.6
  199.6 3.5 collective-permute-start.9
  203.1 1.7 collective-permute-done.8
  204.8 12.7 %collective-permute-start.10 = (f32[4,16,128]{2,1,0:T(8,128)S(1)}, f32[4,16,128]{2,1,0:T(8,128)S(1)}, u32[]{:S(2)}, u32[]{:S(2)}) collective-permute-start(f32[4,16,128]{2,1,0:T(8,128)S(1)} %collective-permute-done.8), channel_id=1, source_target_pairs={{0,1},{1,2},{2,3},{3,4},{4,5},{5,6},{6,7},{7,0},{8,9},{9,10},{10,1... | collective-permute-start | bytes 98312 | tf_op jit(solution)/shard_map/ppermute | solution.py:77
  230.2 3.1 multiply_add_fusion.13
  247.2 1.6 collective-permute-done.11
  250.3 2.0 collective-permute-start.13
  252.4 1.6 collective-permute-done.12
  254.8 2.7 collective-permute-start.15
  257.5 1.5 collective-permute-done.14
  259.1 3.5 collective-permute-start.17
  262.7 1.5 collective-permute-done.16
  264.3 5.1 collective-permute-done.18
  280.6 4.6 reduce-scatter.4.cloned.1.call-done
  286.0 3.4 collective-permute-start
  305.1 3.5 collective-permute-start.21
  308.7 1.7 collective-permute-done.20
  310.4 3.6 collective-permute-start.23
  314.0 1.6 collective-permute-done.22
  315.6 3.6 collective-permute-start.25
  319.2 1.6 collective-permute-done.24
  320.8 5.1 collective-permute-done.26
  338.1 4.8 collective-permute-start.1
  343.0 4.4 convolution_convert_fusion
  347.3 4.6 all-to-all-start.2
  364.7 34.3 %reduce-scatter.8.cloned.1.call-done = bf16[4,16,128]{2,1,0:T(8,128)(2,1)} async-done(((bf16[4,128,128]{2,1,0:T(8,128)(2,1)}), bf16[4,16,128]{2,1,0:T(8,128)(2,1)}) %reduce-scatter.8.cloned.1.call-update) | async-done | bytes 16400 | tf_op jit(solution)/shard_map/reduce_scatter | solution.py:57
  399.7 3.4 collective-permute-start.2
  403.1 1.6 collective-permute-done.2
  412.8 34.4 %all-to-all-done.2 = bf16[8,2048,128]{2,1,0:T(8,128)(2,1)} async-done(((bf16[8,2048,128]{2,1,0:T(8,128)(2,1)}), bf16[8,2048,128]{2,1,0:T(8,128)(2,1)}, u32[]{:S(2)}, u32[]{:S(2)}) %all-to-all-start.2) | async-done | bytes 4194336 | tf_op jit(solution)/shard_map/all_to_all | solution.py:156
  447.2 30.7 %gather_fusion = bf16[8192,128]{1,0:T(8,128)(2,1)} fusion(bf16[16384,128]{1,0:T(8,128)(2,1)} %bitcast.14, s32[8192]{0:T(1024)S(1)} %broadcast_clamp_fusion), kind=kCustom, calls=%fused_computation | custom fusion | bytes 4227072 | tf_op jit(solution)/shard_map/gather | solution.py:157
  477.9 11.8 %convolution_multiply_fusion.1 = f32[1024,128]{1,0:T(8,128)} fusion(bf16[8192,1024]{1,0:T(8,128)(2,1)} %get-tuple-element.83, bf16[8192,128]{1,0:T(8,128)(2,1)} %gather_fusion), kind=kOutput, calls=%fused_computation.20 | convolution fusion | flops 2147614720 | bytes 19398656 | tf_op jit(solution)/shard_map/dot_general | solution.py:158
  489.7 21.9 %fusion.84 = (f32[1024]{0:T(1024)S(1)}, bf16[8192,1024]{1,0:T(8,128)(2,1)}) fusion(f32[8192,1024]{1,0:T(8,128)} %get-tuple-element.84, f32[1024]{0:T(1024)S(1)} %copy-done.6, bf16[8192,128]{1,0:T(8,128)(2,1)S(1)} %copy-done.1, bf16[1024,128]{1,0:T(8,128)(2,1)S(1)} %copy-done.5), kind=kOutput, calls=%fused_computation.320 | convolution fusion | flops 2248145920 | bytes 52699136 | tf_op jit(solution)/shard_map/dot_general | solution.py:161
  511.6 8.9 %fusion.10 = f32[128,1024]{0,1:T(8,128)} fusion(bf16[8192,128]{1,0:T(8,128)(2,1)S(1)} %copy-done, bf16[8192,1024]{1,0:T(8,128)(2,1)} %get-tuple-element.87), kind=kOutput, calls=%fused_computation.19 | convolution fusion | flops 2147483648 | bytes 19398656 | tf_op jit(solution)/shard_map/dot_general | solution.py:167
  524.8 38.0 %psum.22 = f32[1024]{0:T(1024)} all-reduce(f32[1024]{0:T(1024)S(1)} %get-tuple-element.86), channel_id=1, replica_groups=mesh['section'=4,'tile'=8] {'section','tile'}, use_global_device_ids=true, to_apply=%region_10.11 | all-reduce | flops 1024 | bytes 8192 | tf_op jit(solution)/shard_map/psum | solution.py:173
  562.8 87.6 %all-reduce.122.cloned.1.call-done = (f32[128,1024]{0,1:T(8,128)}, f32[1024,128]{1,0:T(8,128)}) async-done(((f32[128,1024]{0,1:T(8,128)}, f32[1024,128]{1,0:T(8,128)}), (f32[128,1024]{0,1:T(8,128)}, f32[1024,128]{1,0:T(8,128)})) %all-reduce.122.cloned.1.call-update) | async-done | bytes 1048592 | tf_op jit(solution)/shard_map/psum | solution.py:173
  650.4 2.0 copy.99
  652.5 1.9 copy.225
  (588 shorter events, 114.1 us)
Async XLA Ops:
  7.2 54.2 %copy-start = (bf16[8192,128]{1,0:T(8,128)(2,1)S(1)}, bf16[8192,128]{1,0:T(8,128)(2,1)}, u32[]{:S(2)}) copy-start(bf16[8192,128]{1,0:T(8,128)(2,1)} %param.10) | copy-start | bytes 6291460
  7.2 52.6 %copy-start.2 = (f32[4,16,128]{2,1,0:T(8,128)S(1)}, f32[4,16,128]{2,1,0:T(8,128)}, u32[]{:S(2)}) copy-start(f32[4,16,128]{2,1,0:T(8,128)} %param.19) | copy-start | bytes 98308
  7.2 54.2 %copy-start.4 = (bf16[128,1024]{1,0:T(8,128)(2,1)S(1)}, bf16[128,1024]{1,0:T(8,128)(2,1)}, u32[]{:S(2)}) copy-start(bf16[128,1024]{1,0:T(8,128)(2,1)} %param.11) | copy-start | bytes 786436
  7.2 54.2 %copy-start.6 = (f32[1024]{0:T(1024)S(1)}, f32[1024]{0:T(1024)}, u32[]{:S(2)}) copy-start(f32[1024]{0:T(1024)} %param.12) | copy-start | bytes 12292
  44.3 72.1 %all-to-all-start = ((s32[8,2048,1]{1,2,0:T(1,128)}), s32[8,2048,1]{1,2,0:T(1,128)S(1)}, u32[]{:S(2)}, u32[]{:S(2)}) async-start(s32[8,2048,1]{1,2,0:T(1,128)} %bitcast.5), calls=%async_computation | async-start | bytes 131072 | tf_op jit(solution)/shard_map/all_to_all | solution.py:134
  116.4 102.0 %copy-start.3 = (s32[4,16]{1,0:T(4,128)S(1)}, s32[4,16]{1,0:T(4,128)}, u32[]{:S(2)}) copy-start(s32[4,16]{1,0:T(4,128)} %param.18) | copy-start | bytes 772
  116.4 113.8 %all-to-all-start.1 = ((bf16[8,2048,128]{2,1,0:T(8,128)(2,1)}), bf16[8,2048,128]{2,1,0:T(8,128)(2,1)}, u32[]{:S(2)}, u32[]{:S(2)}) async-start(bf16[8,2048,128]{2,1,0:T(8,128)(2,1)} %bitcast.89), calls=%async_computation.1 | async-start | bytes 8388608 | tf_op jit(solution)/shard_map/all_to_all | solution.py:133
  121.5 163.7 %reduce-scatter.4.cloned.1.call-start = ((), (), s32[]{:S(2)}) async-start(), calls=%async_computation.6 | async-start | bytes 147456 | tf_op jit(solution)/shard_map/reduce_scatter | solution.py:57
  127.2 5.8 collective-permute-start.3
  133.0 61.4 %collective-permute-start.4 = (f32[4,16,128]{2,1,0:T(8,128)S(1)}, f32[4,16,128]{2,1,0:T(8,128)S(1)}, u32[]{:S(2)}, u32[]{:S(2)}) collective-permute-start(f32[4,16,128]{2,1,0:T(8,128)S(1)} %collective-permute-done.3), channel_id=1, source_target_pairs={{0,1},{1,2},{2,3},{3,4},{4,5},{5,6},{6,7},{7,0},{8,9},{9,10},{10,1... | collective-permute-start | bytes 98312 | tf_op jit(solution)/shard_map/ppermute | solution.py:77
  133.0 61.4 %collective-permute-start.5 = (f32[4,16,128]{2,1,0:T(8,128)S(1)}, f32[4,16,128]{2,1,0:T(8,128)S(1)}, u32[]{:S(2)}, u32[]{:S(2)}) collective-permute-start(f32[4,16,128]{2,1,0:T(8,128)S(1)} %collective-permute-done.3), channel_id=1, source_target_pairs={{0,7},{1,0},{2,1},{3,2},{4,3},{5,4},{6,5},{7,6},{8,15},{9,8},{10,9... | collective-permute-start | bytes 98312 | tf_op jit(solution)/shard_map/ppermute | solution.py:82
  194.3 5.2 collective-permute-start.6
  194.3 5.2 collective-permute-start.7
  199.6 5.2 collective-permute-start.8
  199.6 18.4 %collective-permute-start.9 = (f32[4,16,128]{2,1,0:T(8,128)S(1)}, f32[4,16,128]{2,1,0:T(8,128)S(1)}, u32[]{:S(2)}, u32[]{:S(2)}) collective-permute-start(f32[4,16,128]{2,1,0:T(8,128)S(1)} %collective-permute-done.7), channel_id=1, source_target_pairs={{0,7},{1,0},{2,1},{3,2},{4,3},{5,4},{6,5},{7,6},{8,15},{9,8},{10,9... | collective-permute-start | bytes 98312 | tf_op jit(solution)/shard_map/ppermute | solution.py:82
  204.8 13.6 %collective-permute-start.10 = (f32[4,16,128]{2,1,0:T(8,128)S(1)}, f32[4,16,128]{2,1,0:T(8,128)S(1)}, u32[]{:S(2)}, u32[]{:S(2)}) collective-permute-start(f32[4,16,128]{2,1,0:T(8,128)S(1)} %collective-permute-done.8), channel_id=1, source_target_pairs={{0,1},{1,2},{2,3},{3,4},{4,5},{5,6},{6,7},{7,0},{8,9},{9,10},{10,1... | collective-permute-start | bytes 98312 | tf_op jit(solution)/shard_map/ppermute | solution.py:77
  243.0 5.8 collective-permute-start.11
  247.1 90.3 %reduce-scatter.6.cloned.1.call-start = ((), (), s32[]{:S(2)}) async-start(), calls=%async_computation.7 | async-start | bytes 147456 | tf_op jit(solution)/shard_map/reduce_scatter | solution.py:57
  248.8 5.1 collective-permute-start.12
  250.3 4.5 collective-permute-start.13
  253.9 5.1 collective-permute-start.14
  254.8 4.3 collective-permute-start.15
  259.1 5.1 collective-permute-start.16
  259.1 5.1 collective-permute-start.17
  264.2 5.1 collective-permute-start.18
  286.0 5.0 collective-permute-start
  296.2 8.9 %collective-permute-start.19 = (f32[4,16,128]{2,1,0:T(8,128)S(1)}, f32[4,16,128]{2,1,0:T(8,128)S(1)}, u32[]{:S(2)}, u32[]{:S(2)}) collective-permute-start(f32[4,16,128]{2,1,0:T(8,128)S(1)} %get-tuple-element.69), channel_id=1, source_target_pairs={{8,0},{16,8},{24,16},{9,1},{17,9},{25,17},{10,2},{18,10},{26,18},{... | collective-permute-start | bytes 98312 | tf_op jit(solution)/shard_map/ppermute | solution.py:10
  305.1 5.3 collective-permute-start.20
  305.1 5.2 collective-permute-start.21
  310.4 5.2 collective-permute-start.22
  310.4 5.2 collective-permute-start.23
  315.6 5.2 collective-permute-start.24
  315.6 5.2 collective-permute-start.25
  320.8 5.2 collective-permute-start.26
  338.1 13.9 %collective-permute-start.1 = (f32[4,16,128]{2,1,0:T(8,128)S(1)}, f32[4,16,128]{2,1,0:T(8,128)S(1)}, u32[]{:S(2)}, u32[]{:S(2)}) collective-permute-start(f32[4,16,128]{2,1,0:T(8,128)S(1)} %convert_element_type.63), channel_id=1, source_target_pairs={{0,8},{8,16},{16,24},{1,9},{9,17},{17,25},{2,10},{10,18},{18,26},{... | collective-permute-start | bytes 98312 | tf_op jit(solution)/shard_map/ppermute | solution.py:10
  347.3 99.8 %all-to-all-start.2 = ((bf16[8,2048,128]{2,1,0:T(8,128)(2,1)}), bf16[8,2048,128]{2,1,0:T(8,128)(2,1)}, u32[]{:S(2)}, u32[]{:S(2)}) async-start(bf16[8,2048,128]{2,1,0:T(8,128)(2,1)} %bitcast.88), calls=%async_computation.5 | async-start | bytes 8388608 | tf_op jit(solution)/shard_map/all_to_all | solution.py:156
  351.9 47.0 %reduce-scatter.8.cloned.1.call-start = ((), (), s32[]{:S(2)}) async-start(), calls=%async_computation.8 | async-start | bytes 147456 | tf_op jit(solution)/shard_map/reduce_scatter | solution.py:57
  364.7 285.8 %all-reduce.122.cloned.1.call-start = ((), (), s32[]{:S(2)}) async-start(), calls=%async_computation.9 | async-start | bytes 2097152 | tf_op jit(solution)/shard_map/psum | solution.py:173
  399.7 5.0 collective-permute-start.2
  477.9 11.8 %copy-start.1 = (bf16[8192,128]{1,0:T(8,128)(2,1)S(1)}, bf16[8192,128]{1,0:T(8,128)(2,1)}, u32[]{:S(2)}) copy-start(bf16[8192,128]{1,0:T(8,128)(2,1)} %gather_fusion) | copy-start | bytes 6291460
  477.9 11.8 %copy-start.5 = (bf16[1024,128]{1,0:T(8,128)(2,1)S(1)}, bf16[1024,128]{1,0:T(8,128)(2,1)}, u32[]{:S(2)}) copy-start(bf16[1024,128]{1,0:T(8,128)(2,1)} %param.13) | copy-start | bytes 786436
Sparse Core Ops, SparseCore 0:
  247.3 37.9 reduce-scatter.3
  305.2 31.2 reduce-scatter.5
  364.8 34.1 reduce-scatter.7
  520.6 129.7 all-reduce.121
